TPU v7x, 32 devices: a whole 2x2x4 slice. The times are simulated.
32 devices in a mesh: group: 4 (over x, core), member: 8 (over z, y).
Axes of the slice: x: 2, y: 2, z: 4, core: 2. Of those that a mesh axis runs over, the one named last changes fastest.
Arguments:
- activations: bfloat16 [8192, 1152], P(('group', 'member')), may hold values from -6 to 6
- routes: int32 [8192, 1], P(('group', 'member')), may hold values from 0 to 31; in each aligned block of 256 rows (0 to 255, 256 to 511, ...) at most 16 rows name the same one
- centre_bias: float32 [1152], replicated, may hold values from -2 to 2
- centre_first: float32 [1152], replicated, may hold values from -600 to 600
- centre_second: float32 [1152], replicated, may hold values from 1000 to 1000000
- router: bfloat16 [32, 1152], P(('group', 'member')), may hold values from -0.1875 to 0.1875
- router_first: float32 [32, 1152], P(('group', 'member')), may hold values from -180 to 180
- router_second: float32 [32, 1152], P(('group', 'member')), may hold values from 100 to 100000
- encoder: bfloat16 [32, 1152, 512], P(('group', 'member')), may hold values from -0.1875 to 0.1875
- enc_bias: float32 [32, 512], P(('group', 'member')), may hold values from -3 to 3
- decoder: bfloat16 [32, 512, 1152], P(('group', 'member')), may hold values from -0.25 to 0.25
- encoder_first: float32 [32, 1152, 512], P(('group', 'member')), may hold values from -30 to 30
- encoder_second: float32 [32, 1152, 512], P(('group', 'member')), may hold values from 1 to 1000
- enc_bias_first: float32 [32, 512], P(('group', 'member')), may hold values from -60 to 60
- enc_bias_second: float32 [32, 512], P(('group', 'member')), may hold values from 10 to 10000
- decoder_first: float32 [32, 512, 1152], P(('group', 'member')), may hold values from -30 to 30
- decoder_second: float32 [32, 512, 1152], P(('group', 'member')), may hold values from 1 to 1000
Outputs:
- recon: bfloat16 [8192, 1152], P(('group', 'member'))
- new_centre: float32 [1152], replicated
- new_centre_first: float32 [1152], replicated
- new_centre_second: float32 [1152], replicated
- new_router: bfloat16 [32, 1152], P(('group', 'member'))
- new_router_first: float32 [32, 1152], P(('group', 'member'))
- new_router_second: float32 [32, 1152], P(('group', 'member'))
- new_encoder: bfloat16 [32, 1152, 512], P(('group', 'member'))
- new_enc_bias: float32 [32, 512], P(('group', 'member'))
- new_decoder: bfloat16 [32, 512, 1152], P(('group', 'member'))
- new_encoder_first: float32 [32, 1152, 512], P(('group', 'member'))
- new_encoder_second: float32 [32, 1152, 512], P(('group', 'member'))
- new_enc_bias_first: float32 [32, 512], P(('group', 'member'))
- new_enc_bias_second: float32 [32, 512], P(('group', 'member'))
- new_decoder_first: float32 [32, 512, 1152], P(('group', 'member'))
- new_decoder_second: float32 [32, 512, 1152], P(('group', 'member'))
Inputs may be any that keep to these rules, and one draw needn't show every extreme that they name: `routes`: each row names the one expert that serves it. At most 16 rows of one device name the same expert, and in every draw some device's rows name some expert exactly 16 times.
All inputs are finite; a program needn't handle non-finite values.
Results may differ from a plain program's by a relative error of at most 0.009.
Values may be sent and summed in bfloat16 or wider, within the bound.
A program may use at most 128 MiB of HBM per device.

v0:
```python
import jax
import jax.numpy as jnp
from jax import lax
from jax.sharding import PartitionSpec as P

STEP = 10
learn_rate = 0.001
beta_one = 0.9
beta_two = 0.999
adam_eps = 1e-08
sparsity = 0.1


def adam_update(weights_in, gradient, moment_one, moment_two):
    first_new = beta_one * moment_one + (1.0 - beta_one) * gradient
    second_new = beta_two * moment_two + (1.0 - beta_two) * gradient * gradient
    first_hat = first_new / (1.0 - beta_one**STEP)
    second_hat = second_new / (1.0 - beta_two**STEP)
    stepped = weights_in.astype(jnp.float32) - learn_rate * first_hat / (
        jnp.sqrt(second_hat) + adam_eps
    )
    return (stepped.astype(weights_in.dtype), first_new, second_new)


def forward_pass(in_rows, centre_bias, router_row, encoder, enc_bias, decoder):
    centred = (in_rows.astype(jnp.float32) - centre_bias).astype(jnp.bfloat16)
    preact = jnp.dot(centred, encoder, preferred_element_type=jnp.float32) + enc_bias
    positive = jnp.maximum(preact, 0.0)
    latents = (positive * positive).astype(jnp.bfloat16)
    logits = jnp.dot(in_rows, router_row, preferred_element_type=jnp.float32)
    gating = jax.nn.sigmoid(logits)
    ungated = jnp.dot(latents, decoder, preferred_element_type=jnp.float32)
    rebuilt = centre_bias + gating[:, None] * ungated
    return (centred, positive, latents, gating, ungated, rebuilt)


def backward_pass(
    in_rows, live_mask, centred, positive, latents, gating, ungated, rebuilt, encoder, decoder
):
    errors = (in_rows.astype(jnp.float32) - rebuilt) * live_mask[:, None]
    backward = (-gating[:, None] * errors).astype(jnp.bfloat16)
    decoder_grad = jnp.dot(latents.T, backward, preferred_element_type=jnp.float32)
    latent_grad = jnp.dot(backward, decoder.T, preferred_element_type=jnp.float32) + sparsity
    preact_grad = (latent_grad * 2.0 * positive * live_mask[:, None]).astype(jnp.bfloat16)
    encoder_grad = jnp.dot(centred.T, preact_grad, preferred_element_type=jnp.float32)
    bias_grad = jnp.sum(preact_grad.astype(jnp.float32), axis=0)
    logit_grad = (-jnp.sum(errors * ungated, axis=1) * gating * (1.0 - gating)).astype(jnp.bfloat16)
    router_grad = jnp.dot(logit_grad, in_rows, preferred_element_type=jnp.float32)
    centre_part = -jnp.sum(errors, axis=0) - jnp.dot(
        encoder.astype(jnp.float32), bias_grad, precision=lax.Precision.HIGHEST
    )
    return (encoder_grad, bias_grad, decoder_grad, router_grad, centre_part)


def per_device(
    activations,
    routes,
    centre_bias,
    centre_first,
    centre_second,
    router,
    router_first,
    router_second,
    encoder,
    enc_bias,
    decoder,
    encoder_first,
    encoder_second,
    enc_bias_first,
    enc_bias_second,
    decoder_first,
    decoder_second,
):
    groups = lax.axis_size("group")
    members = lax.axis_size("member")
    devices = groups * members
    row_count = activations.shape[0]
    feature_count = activations.shape[1]
    slot_cap = 2 * row_count // devices
    route_ids = routes[:, 0]
    onehot = (route_ids[:, None] == jnp.arange(devices, dtype=jnp.int32)[None, :]).astype(
        jnp.float32
    )
    earlier = (jnp.arange(row_count)[:, None] > jnp.arange(row_count)[None, :]).astype(jnp.float32)
    before = jnp.dot(earlier, onehot, precision=lax.Precision.HIGHEST)
    slot_rank = jnp.sum(before * onehot, axis=1).astype(jnp.int32)
    position = route_ids * slot_cap + slot_rank
    packed = (
        jnp.zeros((devices * slot_cap, feature_count), jnp.bfloat16).at[position].set(activations)
    )
    filled = (
        jnp.zeros((devices * slot_cap,), jnp.bfloat16)
        .at[position]
        .set(jnp.ones((row_count,), jnp.bfloat16))
    )
    arrived, arrived_mask = (
        lax.all_to_all(
            packed.reshape(devices, slot_cap, feature_count),
            ("group", "member"),
            split_axis=0,
            concat_axis=0,
            tiled=True,
        ),
        lax.all_to_all(
            filled.reshape(devices, slot_cap),
            ("group", "member"),
            split_axis=0,
            concat_axis=0,
            tiled=True,
        ),
    )
    in_rows = arrived.reshape(devices * slot_cap, feature_count)
    live_mask = arrived_mask.reshape(devices * slot_cap).astype(jnp.float32)
    centred, positive, latents, gating, ungated, rebuilt = forward_pass(
        in_rows, centre_bias, router[0], encoder[0], enc_bias[0], decoder[0]
    )
    outgoing = rebuilt.astype(jnp.bfloat16)
    returned = lax.all_to_all(
        outgoing.reshape(devices, slot_cap, feature_count),
        ("group", "member"),
        split_axis=0,
        concat_axis=0,
        tiled=True,
    )
    recon = returned.reshape(devices * slot_cap, feature_count)[position]
    encoder_grad, bias_grad, decoder_grad, router_grad, centre_part = backward_pass(
        in_rows,
        live_mask,
        centred,
        positive,
        latents,
        gating,
        ungated,
        rebuilt,
        encoder[0],
        decoder[0],
    )
    router_new = adam_update(router[0], router_grad, router_first[0], router_second[0])
    encoder_new = adam_update(encoder[0], encoder_grad, encoder_first[0], encoder_second[0])
    bias_new = adam_update(enc_bias[0], bias_grad, enc_bias_first[0], enc_bias_second[0])
    decoder_new = adam_update(decoder[0], decoder_grad, decoder_first[0], decoder_second[0])
    centre_total = lax.psum(centre_part, ("group", "member"))
    centre_new = adam_update(centre_bias, centre_total, centre_first, centre_second)
    return (
        recon,
        centre_new[0],
        centre_new[1],
        centre_new[2],
        router_new[0][None],
        router_new[1][None],
        router_new[2][None],
        encoder_new[0][None],
        bias_new[0][None],
        decoder_new[0][None],
        encoder_new[1][None],
        encoder_new[2][None],
        bias_new[1][None],
        bias_new[2][None],
        decoder_new[1][None],
        decoder_new[2][None],
    )


def solution(mesh):
    placed = (
        P(("group", "member"), None),
        P(("group", "member"), None),
        P(),
        P(),
        P(),
        P(("group", "member"), None),
        P(("group", "member"), None),
        P(("group", "member"), None),
        P(("group", "member"), None, None),
        P(("group", "member"), None),
        P(("group", "member"), None, None),
        P(("group", "member"), None, None),
        P(("group", "member"), None, None),
        P(("group", "member"), None),
        P(("group", "member"), None),
        P(("group", "member"), None, None),
        P(("group", "member"), None, None),
    )
    return jax.shard_map(
        per_device,
        mesh=mesh,
        in_specs=placed,
        out_specs=(
            P(("group", "member"), None),
            P(),
            P(),
            P(),
            P(("group", "member"), None),
            P(("group", "member"), None),
            P(("group", "member"), None),
            P(("group", "member"), None, None),
            P(("group", "member"), None),
            P(("group", "member"), None, None),
            P(("group", "member"), None, None),
            P(("group", "member"), None, None),
            P(("group", "member"), None),
            P(("group", "member"), None),
            P(("group", "member"), None, None),
            P(("group", "member"), None, None),
        ),
        check_vma=False,
    )
```

profile of v0, /device:TPU:0, one launch (start us, length us, event | category | flops | bytes accessed | tf_op | source)
XLA Modules:
  0.0 127.9 jit_solution(12452941034543054141)
XLA Ops:
  0.7 1.0 fusion.22
  1.6 0.7 compare_select_fusion
  2.3 2.2 %scatter_custom_fusion.1 = bf16[512]{0:T(512)(128)(2,1)S(1)} fusion(s32[256]{0:T(256)S(1)} %bitcast.95, bf16[256]{0:T(256)(128)(2,1)S(1)} %broadcast.120, bf16[]{:T(256)} %constant.17.clone.1), kind=kCustom, calls=%fused_computation.76 | custom fusion | bytes 1026 | tf_op jit(solution)/shard_map/scatter | solution.py:94
  4.5 0.7 all_to_all.16
  5.2 7.3 %all-to-all-start.2 = ((bf16[32,1,16]{2,1,0:T(2,128)(2,1)}), bf16[32,1,16]{2,1,0:T(2,128)(2,1)S(1)}, u32[]{:S(2)}, u32[]{:S(2)}) async-start(bf16[32,1,16]{2,1,0:T(2,128)(2,1)} %all_to_all.16), calls=%async_computation.2 | async-start | bytes 32768 | tf_op jit(solution)/shard_map/all_to_all | solution.py:104
  12.5 3.4 %scatter_custom_fusion = bf16[512,1152]{1,0:T(8,128)(2,1)} fusion(s32[256]{0:T(256)S(1)} %bitcast.96, bf16[256,1152]{1,0:T(8,128)(2,1)} %param.17, bf16[]{:T(256)} %constant.17.clone.1), kind=kCustom, calls=%fused_computation.48 | custom fusion | bytes 1180160 | tf_op jit(solution)/shard_map/scatter | solution.py:89
  15.9 3.7 %all-to-all-done.2 = bf16[32,1,16]{2,1,0:T(2,128)(2,1)S(1)} async-done(((bf16[32,1,16]{2,1,0:T(2,128)(2,1)}), bf16[32,1,16]{2,1,0:T(2,128)(2,1)S(1)}, u32[]{:S(2)}, u32[]{:S(2)}) %all-to-all-start.2) | async-done | bytes 1056 | tf_op jit(solution)/shard_map/all_to_all | solution.py:104
  19.6 2.7 %all-to-all-start = ((bf16[32,16,1152]{2,1,0:T(8,128)(2,1)}), bf16[32,16,1152]{2,1,0:T(8,128)(2,1)S(1)}, u32[]{:S(2)}, u32[]{:S(2)}) async-start(bf16[32,16,1152]{2,1,0:T(8,128)(2,1)} %bitcast.3), calls=%async_computation | async-start | bytes 2359296 | tf_op jit(solution)/shard_map/all_to_all | solution.py:97
  22.3 0.6 reduce.2
  23.5 0.6 multiply_reduce_fusion.1
  24.3 28.3 %all-to-all-done = bf16[32,16,1152]{2,1,0:T(8,128)(2,1)S(1)} async-done(((bf16[32,16,1152]{2,1,0:T(8,128)(2,1)}), bf16[32,16,1152]{2,1,0:T(8,128)(2,1)S(1)}, u32[]{:S(2)}, u32[]{:S(2)}) %all-to-all-start) | async-done | bytes 1179680 | tf_op jit(solution)/shard_map/all_to_all | solution.py:97
  53.3 0.9 fusion.8
  54.5 3.2 %multiply_reduce_fusion = (f32[512]{0:T(512)S(1)}, f32[1152]{0:T(1024)}, bf16[512,1152]{1,0:T(8,128)(2,1)}, bf16[512,1152]{1,0:T(8,128)(2,1)}) fusion(f32[512]{0:T(512)S(1)} %reshape.108, f32[512]{0:T(512)S(1)} %get-tuple-element.28, f32[1152]{0:T(1024)S(1)} %copy-done.1, bf16[32,16,1152]{2,1,0:T(8,128)(2,1)S(1)} %all-to-all-done, ...), kind=kOutput, calls=%fused_computation.15 | convolution fusion | flops 610990464 | bytes 5784576 | tf_op jit(solution)/shard_map/dot_general | solution.py:32
  58.1 2.7 %all-to-all-start.1 = ((bf16[32,16,1152]{2,1,0:T(8,128)(2,1)}), bf16[32,16,1152]{2,1,0:T(8,128)(2,1)S(1)}, u32[]{:S(2)}, u32[]{:S(2)}) async-start(bf16[32,16,1152]{2,1,0:T(8,128)(2,1)} %bitcast.90), calls=%async_computation.1 | async-start | bytes 2359296 | tf_op jit(solution)/shard_map/all_to_all | solution.py:118
  60.8 3.7 %convert_reduce_fusion = (f32[512]{0:T(512)S(1)}, bf16[512,512]{1,0:T(8,128)(2,1)}) fusion(f32[512]{0:T(512)} %copy-done.11, f32[512,512]{1,0:T(8,128)} %copy-done.15, bf16[512,1152]{1,0:T(8,128)(2,1)} %get-tuple-element.35, bf16[1,512,1152]{2,1,0:T(8,128)(2,1)} %param.27), kind=kOutput, calls=%fused_computation.42 | convolution fusion | flops 605814272 | bytes 3936256 | tf_op jit(solution)/shard_map/dot_general | solution.py:43
  64.5 1.0 fusion.23
  65.6 0.6 broadcast_in_dim.54
  67.4 0.6 negate_subtract_fusion
  68.0 41.9 %psum.7 = f32[1152]{0:T(1024)S(1)} all-reduce(f32[1152]{0:T(1024)} %negate_subtract_fusion), channel_id=1, replica_groups=mesh['group'=4,'member'=8] {'group','member'}, use_global_device_ids=true, to_apply=%region_5.0 | all-reduce | flops 1152 | bytes 9216 | tf_op jit(solution)/shard_map/psum | solution.py:142
  109.9 1.3 %divide_subtract_fusion.1 = (f32[1,512]{1,0:T(1,128)}, f32[1,512]{1,0:T(1,128)}, f32[1,512]{1,0:T(1,128)}) fusion(f32[1,512]{1,0:T(1,128)} %param.26, f32[1,512]{1,0:T(1,128)} %bitcast.93, f32[1,512]{1,0:T(1,128)} %param.30, f32[1,512]{1,0:T(1,128)} %param.31), kind=kLoop, calls=%fused_computation.72 | loop fusion | flops 6144 | bytes 14336 | tf_op jit(solution)/shard_map/sub | solution.py:19
  111.2 1.3 %divide_subtract_fusion = (f32[1152]{0:T(1024)}, f32[1152]{0:T(1024)}, f32[1152]{0:T(1024)}) fusion(f32[1152]{0:T(1024)S(1)} %copy-done.1, f32[1152]{0:T(1024)S(1)} %psum.7, f32[1152]{0:T(1024)} %param.20, f32[1152]{0:T(1024)} %param.21), kind=kLoop, calls=%fused_computation.61 | loop fusion | flops 13824 | bytes 32256 | tf_op jit(solution)/shard_map/sub | solution.py:19
  112.6 8.3 %fusion.28 = (f32[1,512,1152]{2,1,0:T(8,128)}, bf16[1,512,1152]{2,1,0:T(8,128)(2,1)}, f32[1,512,1152]{2,1,0:T(8,128)}) fusion(f32[1,512,1152]{2,1,0:T(8,128)} %param.33, f32[1,512,1152]{2,1,0:T(8,128)} %param.32, bf16[1,512,1152]{2,1,0:T(8,128)(2,1)} %param.27, bf16[512,1152]{1,0:T(8,128)(2,1)} %get-tuple-element.35, f32[512,512]{1,0:T(8,128)} %copy-done.15), kind=kOutput, calls=%fused_computation.46 | convolution fusion | flops 612761600 | bytes 14024704 | tf_op jit(solution)/shard_map/dot_general | solution.py:42
  120.9 4.8 %fusion.29 = (f32[1,1152,512]{2,1,0:T(8,128)}, bf16[1,1152,512]{2,1,0:T(8,128)(2,1)}, f32[1,1152,512]{2,1,0:T(8,128)}) fusion(f32[1,1152,512]{2,1,0:T(8,128)S(1)} %copy-done.12, f32[1,1152,512]{2,1,0:T(8,128)S(1)} %copy-done.13, bf16[1,1152,512]{2,1,0:T(8,128)(2,1)S(1)} %copy-done, bf16[512,512]{1,0:T(8,128)(2,1)S(1)} %copy-done.16, ...), kind=kOutput, calls=%fused_computation.47 | convolution fusion | flops 614006784 | bytes 13505024 | tf_op jit(solution)/shard_map/dot_general | solution.py:45
  125.7 2.2 %gather_fusion = bf16[256,1152]{1,0:T(8,128)(2,1)} fusion(bf16[512,1152]{1,0:T(8,128)(2,1)S(1)} %bitcast.86, s32[1024]{0:T(1024)} %pad_clamp_fusion), kind=kCustom, calls=%fused_computation | custom fusion | bytes 1180672 | tf_op jit(solution)/shard_map/gather | solution.py:125
  (49 shorter events, 3.3 us)
Async XLA Ops:
  0.6 21.6 %copy-start.4 = (bf16[1,1152]{1,0:T(2,128)(2,1)S(1)}, bf16[1,1152]{1,0:T(2,128)(2,1)}, u32[]{:S(2)}) copy-start(bf16[1,1152]{1,0:T(2,128)(2,1)} %param.22) | copy-start | bytes 6916
  0.7 22.9 %copy-start.8 = (f32[1,1152]{1,0:T(1,128)S(1)}, f32[1,1152]{1,0:T(1,128)}, u32[]{:S(2)}) copy-start(f32[1,1152]{1,0:T(1,128)} %param.24) | copy-start | bytes 13828
  0.7 22.9 %copy-start.9 = (f32[1,1152]{1,0:T(1,128)S(1)}, f32[1,1152]{1,0:T(1,128)}, u32[]{:S(2)}) copy-start(f32[1,1152]{1,0:T(1,128)} %param.23) | copy-start | bytes 13828
  5.2 14.4 %all-to-all-start.2 = ((bf16[32,1,16]{2,1,0:T(2,128)(2,1)}), bf16[32,1,16]{2,1,0:T(2,128)(2,1)S(1)}, u32[]{:S(2)}, u32[]{:S(2)}) async-start(bf16[32,1,16]{2,1,0:T(2,128)(2,1)} %all_to_all.16), calls=%async_computation.2 | async-start | bytes 32768 | tf_op jit(solution)/shard_map/all_to_all | solution.py:104
  12.5 40.5 %copy-start.1 = (f32[1152]{0:T(1024)S(1)}, f32[1152]{0:T(1024)}, u32[]{:S(2)}) copy-start(f32[1152]{0:T(1024)} %param.19) | copy-start | bytes 13828
  19.6 33.0 %all-to-all-start = ((bf16[32,16,1152]{2,1,0:T(8,128)(2,1)}), bf16[32,16,1152]{2,1,0:T(8,128)(2,1)S(1)}, u32[]{:S(2)}, u32[]{:S(2)}) async-start(bf16[32,16,1152]{2,1,0:T(8,128)(2,1)} %bitcast.3), calls=%async_computation | async-start | bytes 2359296 | tf_op jit(solution)/shard_map/all_to_all | solution.py:97
  22.3 30.9 %copy-start = (bf16[1,1152,512]{2,1,0:T(8,128)(2,1)S(1)}, bf16[1,1152,512]{2,1,0:T(8,128)(2,1)}, u32[]{:S(2)}) copy-start(bf16[1,1152,512]{2,1,0:T(8,128)(2,1)} %param.25) | copy-start | bytes 3538948
  22.3 30.9 %copy-start.10 = (f32[1,512]{1,0:T(1,128)S(1)}, f32[1,512]{1,0:T(1,128)}, u32[]{:S(2)}) copy-start(f32[1,512]{1,0:T(1,128)} %param.26) | copy-start | bytes 6148
  24.3 29.8 %copy-start.11 = (f32[512]{0:T(512)}, f32[512]{0:T(512)S(1)}, u32[]{:S(2)}) copy-start(f32[512]{0:T(512)S(1)} %reshape.108) | copy-start | bytes 6148
  53.2 1.3 copy-start.14
  54.1 3.7 %copy-start.15 = (f32[512,512]{1,0:T(8,128)}, f32[512,512]{1,0:T(8,128)S(1)}, u32[]{:S(2)}) copy-start(f32[512,512]{1,0:T(8,128)S(1)} %fusion.8) | copy-start | bytes 3145732
  58.1 67.7 %all-to-all-start.1 = ((bf16[32,16,1152]{2,1,0:T(8,128)(2,1)}), bf16[32,16,1152]{2,1,0:T(8,128)(2,1)S(1)}, u32[]{:S(2)}, u32[]{:S(2)}) async-start(bf16[32,16,1152]{2,1,0:T(8,128)(2,1)} %bitcast.90), calls=%async_computation.1 | async-start | bytes 2359296 | tf_op jit(solution)/shard_map/all_to_all | solution.py:118
  60.7 3.7 %copy-start.2 = (f32[1152]{0:T(1024)S(1)}, f32[1152]{0:T(1024)}, u32[]{:S(2)}) copy-start(f32[1152]{0:T(1024)} %get-tuple-element.39) | copy-start | bytes 13828
  60.7 3.7 %copy-start.3 = (f32[1152]{0:T(1024)S(1)}, f32[1152]{0:T(1024)}, u32[]{:S(2)}) copy-start(f32[1152]{0:T(1024)} %get-tuple-element.40) | copy-start | bytes 13828
  60.8 3.7 %copy-start.5 = (bf16[1152]{0:T(1024)(128)(2,1)S(1)}, bf16[1152]{0:T(1024)(128)(2,1)}, u32[]{:S(2)}) copy-start(bf16[1152]{0:T(1024)(128)(2,1)} %reduce.2) | copy-start | bytes 6916
  60.8 6.6 %copy-start.7 = (f32[1152]{0:T(1024)S(1)}, f32[1152]{0:T(1024)}, u32[]{:S(2)}) copy-start(f32[1152]{0:T(1024)} %get-tuple-element.17) | copy-start | bytes 13828
  64.5 2.9 %copy-start.6 = (f32[512]{0:T(512)}, f32[512]{0:T(512)S(1)}, u32[]{:S(2)}) copy-start(f32[512]{0:T(512)S(1)} %get-tuple-element.37) | copy-start | bytes 6148
  112.5 8.3 %copy-start.12 = (f32[1,1152,512]{2,1,0:T(8,128)S(1)}, f32[1,1152,512]{2,1,0:T(8,128)}, u32[]{:S(2)}) copy-start(f32[1,1152,512]{2,1,0:T(8,128)} %param.29) | copy-start | bytes 7077892
  112.5 8.3 %copy-start.13 = (f32[1,1152,512]{2,1,0:T(8,128)S(1)}, f32[1,1152,512]{2,1,0:T(8,128)}, u32[]{:S(2)}) copy-start(f32[1,1152,512]{2,1,0:T(8,128)} %param.28) | copy-start | bytes 7077892
  112.6 8.3 %copy-start.16 = (bf16[512,512]{1,0:T(8,128)(2,1)S(1)}, bf16[512,512]{1,0:T(8,128)(2,1)}, u32[]{:S(2)}) copy-start(bf16[512,512]{1,0:T(8,128)(2,1)} %get-tuple-element.38) | copy-start | bytes 1572868
where the time goes:
time: 129 us; the launch traced here: 128 us
  blocking collectives  41.9 us (32%)
  waiting for transfers between devices  32 us (25%)
  matrix products  23.6 us (18%)
  starting transfers between devices  12.7 us (10%)
  local copies, waits for them, and re-layouts  10.8 us (8%)
  other arithmetic  6.11 us (5%)
    psum x1, blocking collectives, per_device(): centre_total = lax.psum(centre_part, ('group', 'member'))  41.9 us
    all_to_all x1, waiting for transfers between devices, per_device(): lax.all_to_all(packed.reshape(devices, slot_cap, feature_count), ('group'...  28.3 us
    dot_general x1, matrix products, backward_pass(): jnp.dot(latents.T, backward, preferred_element_type=jnp.float32)  8.33 us
    all_to_all x1, starting transfers between devices, per_device(): lax.all_to_all(filled.reshape(devices, slot_cap), ('group', 'member'), sp...  7.33 us
    dot_general x1, matrix products, backward_pass(): jnp.dot(centred.T, preact_grad, preferred_element_type=jnp.float32)  4.83 us
    all_to_all x1, waiting for transfers between devices, per_device(): lax.all_to_all(filled.reshape(devices, slot_cap), ('group', 'member'), sp...  3.7 us
    dot_general x1, matrix products, backward_pass(): jnp.dot(backward, decoder.T, preferred_element_type=jnp.float32) + sparsity  3.69 us
    scatter x1, local copies, waits for them, and re-layouts, per_device(): jnp.zeros((devices * slot_cap, feature_count), jnp.bfloat16).at[position]  3.35 us
  transfers between devices with their start and end apart: 3, of which 2 were waited for; matrix products, arithmetic and copies ran while one was open for 22% of the time, Pallas kernels for 0%

commit v1 on v0

--- a/solution.py
+++ b/solution.py
@@ -2,6 +2,7 @@
 import jax.numpy as jnp
 from jax import lax
 from jax.sharding import PartitionSpec as P
+from jax.lax import psum
 
 STEP = 10
 learn_rate = 0.001
@@ -139,7 +140,8 @@
     encoder_new = adam_update(encoder[0], encoder_grad, encoder_first[0], encoder_second[0])
     bias_new = adam_update(enc_bias[0], bias_grad, enc_bias_first[0], enc_bias_second[0])
     decoder_new = adam_update(decoder[0], decoder_grad, decoder_first[0], decoder_second[0])
-    centre_total = lax.psum(centre_part, ("group", "member"))
+    set_the_row = lambda buf: psum(psum(buf, "member"), "group")
+    centre_total = set_the_row(centre_part)
     centre_new = adam_update(centre_bias, centre_total, centre_first, centre_second)
     return (
         recon,

time: 129 us -> 122 us (0.946)
  blocking collectives: 41.9 us -> 34.7 us
    psum x1 -> x2, blocking collectives: 41.9 us -> 34.7 us  [per_device(): set_the_row = lambda buf: psum(psum(buf, 'member'), 'group')]
  transfers between devices with their start and end apart: 3 -> 3, of which waited for: 2 -> 2; matrix products, arithmetic and copies ran while one was open for 22% -> 23% of each run, Pallas kernels for 0% -> 0%
where the time goes in v1:
time: 122 us; the launch traced here: 120 us
  blocking collectives  34.7 us (28%)
  waiting for transfers between devices  32 us (26%)
  matrix products  23.6 us (19%)
  starting transfers between devices  12.7 us (10%)
  local copies, waits for them, and re-layouts  10.8 us (9%)
  other arithmetic  5.51 us (5%)
    psum x2, blocking collectives, per_device(): set_the_row = lambda buf: psum(psum(buf, 'member'), 'group')  34.7 us
    all_to_all x1, waiting for transfers between devices, per_device(): lax.all_to_all(packed.reshape(devices, slot_cap, feature_count), ('group'...  28.3 us
    dot_general x1, matrix products, backward_pass(): jnp.dot(latents.T, backward, preferred_element_type=jnp.float32)  8.32 us
    all_to_all x1, starting transfers between devices, per_device(): lax.all_to_all(filled.reshape(devices, slot_cap), ('group', 'member'), sp...  7.33 us
    dot_general x1, matrix products, backward_pass(): jnp.dot(centred.T, preact_grad, preferred_element_type=jnp.float32)  4.83 us
    all_to_all x1, waiting for transfers between devices, per_device(): lax.all_to_all(filled.reshape(devices, slot_cap), ('group', 'member'), sp...  3.7 us
    dot_general x1, matrix products, backward_pass(): jnp.dot(backward, decoder.T, preferred_element_type=jnp.float32) + sparsity  3.69 us
    scatter x1, local copies, waits for them, and re-layouts, per_device(): jnp.zeros((devices * slot_cap, feature_count), jnp.bfloat16).at[position]  3.35 us
  transfers between devices with their start and end apart: 3, of which 2 were waited for; matrix products, arithmetic and copies ran while one was open for 23% of the time, Pallas kernels for 0%

profile of v1, /device:TPU:0, one launch (start us, length us, event | category | flops | bytes accessed | tf_op | source)
XLA Modules:
  0.0 120.1 jit_solution(12944510627616030664)
XLA Ops:
  0.7 1.0 fusion.22
  1.6 0.7 compare_select_fusion
  2.3 2.2 %scatter_custom_fusion.1 = bf16[512]{0:T(512)(128)(2,1)S(1)} fusion(s32[256]{0:T(256)S(1)} %bitcast.95, bf16[256]{0:T(256)(128)(2,1)S(1)} %broadcast.120, bf16[]{:T(256)} %constant.17.clone.1), kind=kCustom, calls=%fused_computation.76 | custom fusion | bytes 1026 | tf_op jit(solution)/shard_map/scatter | solution.py:95
  4.5 0.7 all_to_all.16
  5.2 7.3 %all-to-all-start.2 = ((bf16[32,1,16]{2,1,0:T(2,128)(2,1)}), bf16[32,1,16]{2,1,0:T(2,128)(2,1)S(1)}, u32[]{:S(2)}, u32[]{:S(2)}) async-start(bf16[32,1,16]{2,1,0:T(2,128)(2,1)} %all_to_all.16), calls=%async_computation.2 | async-start | bytes 32768 | tf_op jit(solution)/shard_map/all_to_all | solution.py:105
  12.5 3.4 %scatter_custom_fusion = bf16[512,1152]{1,0:T(8,128)(2,1)} fusion(s32[256]{0:T(256)S(1)} %bitcast.96, bf16[256,1152]{1,0:T(8,128)(2,1)} %param.17, bf16[]{:T(256)} %constant.17.clone.1), kind=kCustom, calls=%fused_computation.48 | custom fusion | bytes 1180160 | tf_op jit(solution)/shard_map/scatter | solution.py:90
  15.9 3.7 %all-to-all-done.2 = bf16[32,1,16]{2,1,0:T(2,128)(2,1)S(1)} async-done(((bf16[32,1,16]{2,1,0:T(2,128)(2,1)}), bf16[32,1,16]{2,1,0:T(2,128)(2,1)S(1)}, u32[]{:S(2)}, u32[]{:S(2)}) %all-to-all-start.2) | async-done | bytes 1056 | tf_op jit(solution)/shard_map/all_to_all | solution.py:105
  19.6 2.7 %all-to-all-start = ((bf16[32,16,1152]{2,1,0:T(8,128)(2,1)}), bf16[32,16,1152]{2,1,0:T(8,128)(2,1)S(1)}, u32[]{:S(2)}, u32[]{:S(2)}) async-start(bf16[32,16,1152]{2,1,0:T(8,128)(2,1)} %bitcast.3), calls=%async_computation | async-start | bytes 2359296 | tf_op jit(solution)/shard_map/all_to_all | solution.py:98
  22.3 0.6 reduce.2
  23.5 0.6 multiply_reduce_fusion.1
  24.3 28.3 %all-to-all-done = bf16[32,16,1152]{2,1,0:T(8,128)(2,1)S(1)} async-done(((bf16[32,16,1152]{2,1,0:T(8,128)(2,1)}), bf16[32,16,1152]{2,1,0:T(8,128)(2,1)S(1)}, u32[]{:S(2)}, u32[]{:S(2)}) %all-to-all-start) | async-done | bytes 1179680 | tf_op jit(solution)/shard_map/all_to_all | solution.py:98
  53.3 0.9 fusion.8
  54.5 3.2 %multiply_reduce_fusion = (f32[512]{0:T(512)S(1)}, f32[1152]{0:T(1024)}, bf16[512,1152]{1,0:T(8,128)(2,1)}, bf16[512,1152]{1,0:T(8,128)(2,1)}) fusion(f32[512]{0:T(512)S(1)} %reshape.108, f32[512]{0:T(512)S(1)} %get-tuple-element.28, f32[1152]{0:T(1024)S(1)} %copy-done.1, bf16[32,16,1152]{2,1,0:T(8,128)(2,1)S(1)} %all-to-all-done, ...), kind=kOutput, calls=%fused_computation.15 | convolution fusion | flops 610990464 | bytes 5784576 | tf_op jit(solution)/shard_map/dot_general | solution.py:33
  58.0 2.7 %all-to-all-start.1 = ((bf16[32,16,1152]{2,1,0:T(8,128)(2,1)}), bf16[32,16,1152]{2,1,0:T(8,128)(2,1)S(1)}, u32[]{:S(2)}, u32[]{:S(2)}) async-start(bf16[32,16,1152]{2,1,0:T(8,128)(2,1)} %bitcast.90), calls=%async_computation.1 | async-start | bytes 2359296 | tf_op jit(solution)/shard_map/all_to_all | solution.py:119
  60.8 3.7 %convert_reduce_fusion = (f32[512]{0:T(512)S(1)}, bf16[512,512]{1,0:T(8,128)(2,1)}) fusion(f32[512]{0:T(512)} %copy-done.11, f32[512,512]{1,0:T(8,128)} %copy-done.15, bf16[512,1152]{1,0:T(8,128)(2,1)} %get-tuple-element.35, bf16[1,512,1152]{2,1,0:T(8,128)(2,1)} %param.27), kind=kOutput, calls=%fused_computation.42 | convolution fusion | flops 605814272 | bytes 3936256 | tf_op jit(solution)/shard_map/dot_general | solution.py:44
  64.5 1.0 fusion.23
  65.6 0.6 broadcast_in_dim.54
  67.4 28.7 %psum.14 = f32[1152]{0:T(1024)} all-reduce(f32[1152]{0:T(1024)S(1)} %negate_subtract_fusion), channel_id=1, replica_groups=mesh['group'=4,'member'=8] {'member'}, use_global_device_ids=true, to_apply=%region_5.0 | all-reduce | flops 1152 | bytes 9216 | tf_op jit(solution)/shard_map/psum | solution.py:143
  96.0 6.0 %psum.15 = f32[1152]{0:T(1024)S(1)} all-reduce(f32[1152]{0:T(1024)} %psum.14), channel_id=1, replica_groups=mesh['group'=4,'member'=8] {'group'}, use_global_device_ids=true, to_apply=%region_6.0 | all-reduce | flops 1152 | bytes 9216 | tf_op jit(solution)/shard_map/psum | solution.py:143
  102.1 1.3 %divide_subtract_fusion.1 = (f32[1,512]{1,0:T(1,128)}, f32[1,512]{1,0:T(1,128)}, f32[1,512]{1,0:T(1,128)}) fusion(f32[1,512]{1,0:T(1,128)} %param.26, f32[1,512]{1,0:T(1,128)} %bitcast.93, f32[1,512]{1,0:T(1,128)} %param.30, f32[1,512]{1,0:T(1,128)} %param.31), kind=kLoop, calls=%fused_computation.72 | loop fusion | flops 6144 | bytes 14336 | tf_op jit(solution)/shard_map/sub | solution.py:20
  103.4 1.3 %divide_subtract_fusion = (f32[1152]{0:T(1024)}, f32[1152]{0:T(1024)}, f32[1152]{0:T(1024)}) fusion(f32[1152]{0:T(1024)S(1)} %copy-done.1, f32[1152]{0:T(1024)S(1)} %psum.15, f32[1152]{0:T(1024)} %param.20, f32[1152]{0:T(1024)} %param.21), kind=kLoop, calls=%fused_computation.61 | loop fusion | flops 13824 | bytes 32256 | tf_op jit(solution)/shard_map/sub | solution.py:20
  104.8 8.3 %fusion.28 = (f32[1,512,1152]{2,1,0:T(8,128)}, bf16[1,512,1152]{2,1,0:T(8,128)(2,1)}, f32[1,512,1152]{2,1,0:T(8,128)}) fusion(f32[1,512,1152]{2,1,0:T(8,128)} %param.33, f32[1,512,1152]{2,1,0:T(8,128)} %param.32, bf16[1,512,1152]{2,1,0:T(8,128)(2,1)} %param.27, bf16[512,1152]{1,0:T(8,128)(2,1)} %get-tuple-element.35, f32[512,512]{1,0:T(8,128)} %copy-done.15), kind=kOutput, calls=%fused_computation.46 | convolution fusion | flops 612761600 | bytes 14024704 | tf_op jit(solution)/shard_map/dot_general | solution.py:43
  113.1 4.8 %fusion.29 = (f32[1,1152,512]{2,1,0:T(8,128)}, bf16[1,1152,512]{2,1,0:T(8,128)(2,1)}, f32[1,1152,512]{2,1,0:T(8,128)}) fusion(f32[1,1152,512]{2,1,0:T(8,128)S(1)} %copy-done.12, f32[1,1152,512]{2,1,0:T(8,128)S(1)} %copy-done.13, bf16[1,1152,512]{2,1,0:T(8,128)(2,1)S(1)} %copy-done, bf16[512,512]{1,0:T(8,128)(2,1)S(1)} %copy-done.16, ...), kind=kOutput, calls=%fused_computation.47 | convolution fusion | flops 614006784 | bytes 13505024 | tf_op jit(solution)/shard_map/dot_general | solution.py:46
  117.9 2.2 %gather_fusion = bf16[256,1152]{1,0:T(8,128)(2,1)} fusion(bf16[512,1152]{1,0:T(8,128)(2,1)S(1)} %bitcast.86, s32[1024]{0:T(1024)} %pad_clamp_fusion), kind=kCustom, calls=%fused_computation | custom fusion | bytes 1180672 | tf_op jit(solution)/shard_map/gather | solution.py:126
  (50 shorter events, 3.3 us)
Async XLA Ops:
  0.6 21.6 %copy-start.4 = (bf16[1,1152]{1,0:T(2,128)(2,1)S(1)}, bf16[1,1152]{1,0:T(2,128)(2,1)}, u32[]{:S(2)}) copy-start(bf16[1,1152]{1,0:T(2,128)(2,1)} %param.22) | copy-start | bytes 6916
  0.7 22.9 %copy-start.8 = (f32[1,1152]{1,0:T(1,128)S(1)}, f32[1,1152]{1,0:T(1,128)}, u32[]{:S(2)}) copy-start(f32[1,1152]{1,0:T(1,128)} %param.24) | copy-start | bytes 13828
  0.7 22.9 %copy-start.9 = (f32[1,1152]{1,0:T(1,128)S(1)}, f32[1,1152]{1,0:T(1,128)}, u32[]{:S(2)}) copy-start(f32[1,1152]{1,0:T(1,128)} %param.23) | copy-start | bytes 13828
  5.2 14.4 %all-to-all-start.2 = ((bf16[32,1,16]{2,1,0:T(2,128)(2,1)}), bf16[32,1,16]{2,1,0:T(2,128)(2,1)S(1)}, u32[]{:S(2)}, u32[]{:S(2)}) async-start(bf16[32,1,16]{2,1,0:T(2,128)(2,1)} %all_to_all.16), calls=%async_computation.2 | async-start | bytes 32768 | tf_op jit(solution)/shard_map/all_to_all | solution.py:105
  12.5 40.5 %copy-start.1 = (f32[1152]{0:T(1024)S(1)}, f32[1152]{0:T(1024)}, u32[]{:S(2)}) copy-start(f32[1152]{0:T(1024)} %param.19) | copy-start | bytes 13828
  19.6 33.0 %all-to-all-start = ((bf16[32,16,1152]{2,1,0:T(8,128)(2,1)}), bf16[32,16,1152]{2,1,0:T(8,128)(2,1)S(1)}, u32[]{:S(2)}, u32[]{:S(2)}) async-start(bf16[32,16,1152]{2,1,0:T(8,128)(2,1)} %bitcast.3), calls=%async_computation | async-start | bytes 2359296 | tf_op jit(solution)/shard_map/all_to_all | solution.py:98
  22.3 30.9 %copy-start = (bf16[1,1152,512]{2,1,0:T(8,128)(2,1)S(1)}, bf16[1,1152,512]{2,1,0:T(8,128)(2,1)}, u32[]{:S(2)}) copy-start(bf16[1,1152,512]{2,1,0:T(8,128)(2,1)} %param.25) | copy-start | bytes 3538948
  22.3 30.9 %copy-start.10 = (f32[1,512]{1,0:T(1,128)S(1)}, f32[1,512]{1,0:T(1,128)}, u32[]{:S(2)}) copy-start(f32[1,512]{1,0:T(1,128)} %param.26) | copy-start | bytes 6148
  24.3 29.8 %copy-start.11 = (f32[512]{0:T(512)}, f32[512]{0:T(512)S(1)}, u32[]{:S(2)}) copy-start(f32[512]{0:T(512)S(1)} %reshape.108) | copy-start | bytes 6148
  53.2 1.3 %copy-start.14 = (bf16[1,512,1152]{2,1,0:T(8,128)(2,1)S(1)}, bf16[1,512,1152]{2,1,0:T(8,128)(2,1)}, u32[]{:S(2)}) copy-start(bf16[1,512,1152]{2,1,0:T(8,128)(2,1)} %param.27) | copy-start | bytes 3538948
  54.1 3.6 %copy-start.15 = (f32[512,512]{1,0:T(8,128)}, f32[512,512]{1,0:T(8,128)S(1)}, u32[]{:S(2)}) copy-start(f32[512,512]{1,0:T(8,128)S(1)} %fusion.8) | copy-start | bytes 3145732
  58.0 59.9 %all-to-all-start.1 = ((bf16[32,16,1152]{2,1,0:T(8,128)(2,1)}), bf16[32,16,1152]{2,1,0:T(8,128)(2,1)S(1)}, u32[]{:S(2)}, u32[]{:S(2)}) async-start(bf16[32,16,1152]{2,1,0:T(8,128)(2,1)} %bitcast.90), calls=%async_computation.1 | async-start | bytes 2359296 | tf_op jit(solution)/shard_map/all_to_all | solution.py:119
  60.7 3.7 %copy-start.2 = (f32[1152]{0:T(1024)S(1)}, f32[1152]{0:T(1024)}, u32[]{:S(2)}) copy-start(f32[1152]{0:T(1024)} %get-tuple-element.39) | copy-start | bytes 13828
  60.7 3.7 %copy-start.3 = (f32[1152]{0:T(1024)S(1)}, f32[1152]{0:T(1024)}, u32[]{:S(2)}) copy-start(f32[1152]{0:T(1024)} %get-tuple-element.40) | copy-start | bytes 13828
  60.8 3.7 %copy-start.5 = (bf16[1152]{0:T(1024)(128)(2,1)S(1)}, bf16[1152]{0:T(1024)(128)(2,1)}, u32[]{:S(2)}) copy-start(bf16[1152]{0:T(1024)(128)(2,1)} %reduce.2) | copy-start | bytes 6916
  60.8 6.6 %copy-start.7 = (f32[1152]{0:T(1024)S(1)}, f32[1152]{0:T(1024)}, u32[]{:S(2)}) copy-start(f32[1152]{0:T(1024)} %get-tuple-element.17) | copy-start | bytes 13828
  64.5 2.9 %copy-start.6 = (f32[512]{0:T(512)}, f32[512]{0:T(512)S(1)}, u32[]{:S(2)}) copy-start(f32[512]{0:T(512)S(1)} %get-tuple-element.37) | copy-start | bytes 6148
  104.8 8.3 %copy-start.12 = (f32[1,1152,512]{2,1,0:T(8,128)S(1)}, f32[1,1152,512]{2,1,0:T(8,128)}, u32[]{:S(2)}) copy-start(f32[1,1152,512]{2,1,0:T(8,128)} %param.29) | copy-start | bytes 7077892
  104.8 8.3 %copy-start.13 = (f32[1,1152,512]{2,1,0:T(8,128)S(1)}, f32[1,1152,512]{2,1,0:T(8,128)}, u32[]{:S(2)}) copy-start(f32[1,1152,512]{2,1,0:T(8,128)} %param.28) | copy-start | bytes 7077892
  104.8 8.3 %copy-start.16 = (bf16[512,512]{1,0:T(8,128)(2,1)S(1)}, bf16[512,512]{1,0:T(8,128)(2,1)}, u32[]{:S(2)}) copy-start(bf16[512,512]{1,0:T(8,128)(2,1)} %get-tuple-element.38) | copy-start | bytes 1572868
